TPU v7x, 256 devices: a whole 4x4x8 slice. The times are simulated.
256 devices in a mesh: fsdp: 8 (over x, y_hi), frame: 32 (over y_lo, z, core).
Axes of the slice: x: 4, y: 4 (y_hi: 2, y_lo: 2; y = y_hi * 2 + y_lo), z: 8, core: 2. Of those that a mesh axis runs over, the one named last changes fastest.
Arguments:
- queries: bfloat16 [32, 1024, 1024], P('frame', 'fsdp'), may hold values from -5 to 5
- key_rows: bfloat16 [32, 1024, 1024], P('frame', 'fsdp'), may hold values from -5 to 5
- value_rows: bfloat16 [32, 1024, 1024], P('frame', 'fsdp'), may hold values from -6 to 6
- out_weight: bfloat16 [1024, 2048], P(('fsdp', 'frame')), may hold values from -0.75 to 0.75
- conv_weight: bfloat16 [31, 2048], replicated, may hold values from -1 to 1
- grad_out: bfloat16 [32, 1024, 2048], P('frame', 'fsdp'), may hold values from -6 to 6
Outputs:
- block_out: bfloat16 [32, 1024, 2048], P('frame', 'fsdp')
- grad_queries: bfloat16 [32, 1024, 1024], P('frame', 'fsdp')
- grad_keys: bfloat16 [32, 1024, 1024], P('frame', 'fsdp')
- grad_values: bfloat16 [32, 1024, 1024], P('frame', 'fsdp')
- weight_grad: float32 [1024, 2048], P(('fsdp', 'frame'))
- conv_grad: float32 [31, 2048], replicated
All inputs are finite; a program needn't handle non-finite values.
Results may differ from a plain program's by a relative error of at most 0.014.
Values may be sent and summed in bfloat16 or wider, within the bound.
A program may use at most 128 MiB of HBM per device.

v0:
```python
import math
import jax
import jax.numpy as jnp
from jax import lax
from jax.sharding import PartitionSpec as P

HEADS = 8
HDIM = 128
KERNEL = 31


def with_halo(cells, sides, width):
    for axis, dim in sides:
        count = lax.axis_size(axis)
        ends = count - 1
        head = lax.slice_in_dim(cells, 0, width, axis=dim)
        tail = lax.slice_in_dim(cells, cells.shape[dim] - width, cells.shape[dim], axis=dim)
        cells = jnp.concatenate(
            [
                lax.ppermute(tail, axis, [(i, (i + 1) % count) for i in range(ends)]),
                cells,
                lax.ppermute(head, axis, [((i + 1) % count, i) for i in range(ends)]),
            ],
            axis=dim,
        )
    return cells


def head_scores(queries, key_rows):
    return jnp.einsum("qd,kd->qk", queries, key_rows, preferred_element_type=jnp.float32) * (
        1.0 / math.sqrt(HDIM)
    )


def forward_head(queries, key_rows, value_rows):
    scores = head_scores(queries, key_rows)
    row_max = jnp.max(scores, axis=1)
    exponent = jnp.exp(scores - row_max[:, None])
    row_sum = jnp.sum(exponent, axis=1)
    rounded = (exponent / row_sum[:, None]).astype(jnp.bfloat16)
    attended = jnp.dot(rounded, value_rows, preferred_element_type=jnp.float32).astype(jnp.bfloat16)
    return (attended, row_max, row_sum)


def score_grads(queries, key_rows, value_rows, upstream, row_max, row_sum, row_dot):
    scores = head_scores(queries, key_rows)
    weights = jnp.exp(scores - row_max[:, None]) / row_sum[:, None]
    grad_probs = jnp.einsum("qd,kd->qk", upstream, value_rows, preferred_element_type=jnp.float32)
    if row_dot is None:
        row_dot = jnp.sum(weights * grad_probs, axis=1)
    grad_scores = (weights * (grad_probs - row_dot[:, None])).astype(jnp.bfloat16)
    return (weights, grad_scores, row_dot)


def query_grad(grad_scores, key_rows):
    product = jnp.dot(grad_scores, key_rows, preferred_element_type=jnp.float32)
    return (product * (1.0 / math.sqrt(HDIM))).astype(jnp.bfloat16)


def key_grads(queries, weights, grad_scores, upstream):
    grad_key = jnp.einsum("qk,qd->kd", grad_scores, queries, preferred_element_type=jnp.float32) * (
        1.0 / math.sqrt(HDIM)
    )
    grad_value = jnp.einsum(
        "qk,qd->kd", weights.astype(jnp.bfloat16), upstream, preferred_element_type=jnp.float32
    )
    return (grad_key, grad_value)


def depthwise(signal, taps):
    channels = signal.shape[1]
    result = lax.conv_general_dilated(
        signal[None],
        taps[:, None, :],
        (1,),
        "VALID",
        dimension_numbers=("NWC", "WIO", "NWC"),
        feature_group_count=channels,
        precision=lax.Precision.HIGHEST,
        preferred_element_type=jnp.float32,
    )
    return result[0]


def shards(queries, key_rows, value_rows, out_weight, conv_weight, grad_out):
    local_rows = queries.shape[1]
    half_width = KERNEL // 2
    own_queries = queries[0]
    own_keys = key_rows[0]
    own_values = value_rows[0]
    upstream = grad_out[0].astype(jnp.float32)
    full_weight = lax.all_gather(out_weight, ("fsdp", "frame"), axis=0, tiled=True)
    groups = lax.axis_size("fsdp")
    all_keys, all_values = (
        lax.all_gather(own_keys, "fsdp", axis=0, tiled=True),
        lax.all_gather(own_values, "fsdp", axis=0, tiled=True),
    )
    pieces = []
    maxima = []
    row_sums = []
    for head_index in range(HEADS):
        columns = slice(head_index * HDIM, (head_index + 1) * HDIM)
        attended, row_max, row_sum = forward_head(
            own_queries[:, columns], all_keys[:, columns], all_values[:, columns]
        )
        pieces.append(attended)
        maxima.append(row_max)
        row_sums.append(row_sum)
    attention = jnp.concatenate(pieces, axis=1)
    row_maxes = jnp.stack(maxima, axis=1)
    row_totals = jnp.stack(row_sums, axis=1)
    projected = jnp.dot(attention, full_weight, preferred_element_type=jnp.float32).astype(
        jnp.bfloat16
    )
    padded = with_halo(projected[None], (("fsdp", 1),), half_width)[0].astype(jnp.float32)
    conv_taps = conv_weight.astype(jnp.float32)
    conv_value = depthwise(padded, conv_taps)
    sigmoid_conv = jax.nn.sigmoid(conv_value)
    block_out = (padded[half_width : half_width + local_rows] + conv_value * sigmoid_conv).astype(
        jnp.bfloat16
    )
    grad_conv = (upstream * sigmoid_conv * (1.0 + conv_value * (1.0 - sigmoid_conv))).astype(
        jnp.bfloat16
    )
    grad_padded = with_halo(grad_conv[None], (("fsdp", 1),), half_width)[0].astype(jnp.float32)
    grad_projected = (upstream + depthwise(grad_padded, conv_taps[::-1])).astype(jnp.bfloat16)
    conv_terms = depthwise(padded, grad_conv.astype(jnp.float32))
    total_frames = local_rows * groups * lax.axis_size("frame")
    grad_scale = 1.0 / math.sqrt(total_frames)
    conv_grad = lax.psum(conv_terms, ("fsdp", "frame")) * grad_scale
    weight_grad = (
        lax.psum_scatter(
            jnp.einsum("ri,rd->id", attention, grad_projected, preferred_element_type=jnp.float32),
            ("fsdp", "frame"),
            scatter_dimension=0,
            tiled=True,
        )
        * grad_scale
    )
    grad_attention = jnp.einsum(
        "rd,id->ri", grad_projected, full_weight, preferred_element_type=jnp.float32
    ).astype(jnp.bfloat16)
    query_list = []
    row_dots = []
    for head_index in range(HEADS):
        columns = slice(head_index * HDIM, (head_index + 1) * HDIM)
        weights, grad_scores, row_dot = score_grads(
            own_queries[:, columns],
            all_keys[:, columns],
            all_values[:, columns],
            grad_attention[:, columns],
            row_maxes[:, head_index],
            row_totals[:, head_index],
            None,
        )
        query_list.append(query_grad(grad_scores, all_keys[:, columns]))
        row_dots.append(row_dot)
    row_dot_table = jnp.stack(row_dots, axis=1)
    span_queries, span_grads = (
        lax.all_gather(own_queries, "fsdp", axis=0, tiled=True),
        lax.all_gather(grad_attention, "fsdp", axis=0, tiled=True),
    )
    span_max, span_sum, span_dot = (
        lax.all_gather(row_maxes, "fsdp", axis=0, tiled=True),
        lax.all_gather(row_totals, "fsdp", axis=0, tiled=True),
        lax.all_gather(row_dot_table, "fsdp", axis=0, tiled=True),
    )
    key_list = []
    value_list = []
    for head_index in range(HEADS):
        columns = slice(head_index * HDIM, (head_index + 1) * HDIM)
        weights, grad_scores, unused_dot = score_grads(
            span_queries[:, columns],
            own_keys[:, columns],
            own_values[:, columns],
            span_grads[:, columns],
            span_max[:, head_index],
            span_sum[:, head_index],
            span_dot[:, head_index],
        )
        grad_key, grad_value = key_grads(
            span_queries[:, columns], weights, grad_scores, span_grads[:, columns]
        )
        key_list.append(grad_key.astype(jnp.bfloat16))
        value_list.append(grad_value.astype(jnp.bfloat16))
    grad_queries = jnp.concatenate(query_list, axis=1)
    grad_keys = jnp.concatenate(key_list, axis=1)
    grad_values = jnp.concatenate(value_list, axis=1)
    return (
        block_out[None],
        grad_queries[None],
        grad_keys[None],
        grad_values[None],
        weight_grad,
        conv_grad,
    )


def solution(mesh):
    return jax.shard_map(
        shards,
        mesh=mesh,
        in_specs=(
            P("frame", "fsdp", None),
            P("frame", "fsdp", None),
            P("frame", "fsdp", None),
            P(("fsdp", "frame"), None),
            P(),
            P("frame", "fsdp", None),
        ),
        out_specs=(
            P("frame", "fsdp", None),
            P("frame", "fsdp", None),
            P("frame", "fsdp", None),
            P("frame", "fsdp", None),
            P(("fsdp", "frame"), None),
            P(),
        ),
        check_vma=False,
    )
```

profile of v0, /device:TPU:97, one launch (start us, length us, event | category | flops | bytes accessed | tf_op | source)
XLA Modules:
  0.0 727.7 jit_solution(12551051840050109042)
XLA Ops:
  10.0 7.9 %rev.3 = f32[31,2048]{1,0:T(8,128)} reverse(bf16[31,2048]{1,0:T(8,128)(2,1)} %param.10), dimensions={0} | reverse | bytes 380928 | tf_op jit(solution)/shard_map/rev | solution.py:126
  17.9 53.3 %all-gather.12.cloned.1.call-done = bf16[1,1024,1024]{2,1,0:T(8,128)(2,1)} async-done(((bf16[1,128,1024]{2,1,0:T(8,128)(2,1)}), bf16[1,1024,1024]{2,1,0:T(8,128)(2,1)}) %all-gather.12.cloned.1.call-update) | async-done | bytes 2097168 | tf_op jit(solution)/shard_map/all_gather | solution.py:95
  84.2 27.9 %all_gather.29 = f32[1024,8]{0,1:T(8,128)S(1)} all-gather(f32[128,8]{0,1:T(8,128)S(1)} %stack.7), channel_id=1, replica_groups=mesh['fsdp'=8,'frame'=32] {'fsdp'}, dimensions={0}, use_global_device_ids=true | all-gather | bytes 36864 | tf_op jit(solution)/shard_map/all_gather | solution.py:165
  112.1 28.1 %all_gather.28 = f32[1024,8]{0,1:T(8,128)S(1)} all-gather(f32[128,8]{0,1:T(8,128)S(1)} %stack.6), channel_id=1, replica_groups=mesh['fsdp'=8,'frame'=32] {'fsdp'}, dimensions={0}, use_global_device_ids=true | all-gather | bytes 36864 | tf_op jit(solution)/shard_map/all_gather | solution.py:164
  145.4 49.5 %all-gather.16.cloned.1.call-done = bf16[1,1024,1024]{2,1,0:T(8,128)(2,1)} async-done(((bf16[1,128,1024]{2,1,0:T(8,128)(2,1)}), bf16[1,1024,1024]{2,1,0:T(8,128)(2,1)}) %all-gather.16.cloned.1.call-update) | async-done | bytes 2097168 | tf_op jit(solution)/shard_map/all_gather | solution.py:160
  194.9 2.3 fusion.8
  204.3 109.2 %all-gather.18.cloned.1.call-done = bf16[256,4,2048]{2,1,0:T(4,128)(2,1)} async-done(((bf16[1,4,2048]{2,1,0:T(4,128)(2,1)}), bf16[256,4,2048]{2,1,0:T(4,128)(2,1)}) %all-gather.18.cloned.1.call-update) | async-done | bytes 4194320 | tf_op jit(solution)/shard_map/all_gather | solution.py:92
  313.6 6.9 reshape.105
  320.5 2.9 convolution_convert_fusion
  324.9 5.5 collective-permute-start
  332.7 8.1 %multiply_convert_fusion = (bf16[1,128,2048]{2,0,1:T(2,128)(2,1)S(1)}, f32[1,128,2048]{2,0,1:T(1,128)S(1)}) fusion(bf16[1,128,2048]{2,1,0:T(8,128)(2,1)S(1)} %copy-done.26, bf16[31,1,2048]{2,0,1:T(8,128)(2,1)S(1)} %bitcast.163, bf16[1,158,2048]{2,1,0:T(8,128)(2,1)S(1)} %pad_maximum_fusion), kind=kOutput, calls=%fused_computation.178 | convolution fusion | flops 18874368 | bytes 2871296 | tf_op jit(solution)/shard_map/conv_general_dilated | solution.py:72
  342.4 6.3 collective-permute-start.2
  348.7 7.4 %fusion.119 = f32[1,31,2048]{2,0,1:T(1,128)S(1)} fusion(f32[1,128,2048]{2,0,1:T(1,128)S(1)} %get-tuple-element.65, bf16[1,158,2048]{2,1,0:T(8,128)(2,1)S(1)} %pad_maximum_fusion, bf16[1,128,2048]{2,1,0:T(8,128)(2,1)S(1)} %copy-done.26), kind=kOutput, calls=%fused_computation.176 | convolution fusion | flops 18874368 | bytes 2473984 | tf_op jit(solution)/shard_map/conv_general_dilated | solution.py:72
  358.3 4.9 fusion
  364.2 2.3 convolution_convert_fusion.1
  366.5 2.2 multiply_reduce_fusion.7
  382.7 4.5 fusion.126
  392.1 30.5 %all_gather.31 = f32[1024,8]{0,1:T(8,128)S(1)} all-gather(f32[128,8]{0,1:T(8,128)S(1)} %stack.8), channel_id=1, replica_groups=mesh['fsdp'=8,'frame'=32] {'fsdp'}, dimensions={0}, use_global_device_ids=true | all-gather | bytes 36864 | tf_op jit(solution)/shard_map/all_gather | solution.py:166
  422.6 9.0 %all-gather.10.cloned.1.call-done = bf16[1024,1024]{1,0:T(8,128)(2,1)} async-done(((bf16[128,1024]{1,0:T(8,128)(2,1)}), bf16[1024,1024]{1,0:T(8,128)(2,1)}) %all-gather.10.cloned.1.call-update) | async-done | bytes 2097168 | tf_op jit(solution)/shard_map/all_gather | solution.py:161
  431.7 2.3 fusion.63
  436.0 2.2 fusion.67
  438.2 2.2 fusion.69
  442.6 2.2 fusion.73
  455.4 262.4 %all-reduce.4.cloned.1.call-done = (f32[1024,2048]{1,0:T(8,128)}, f32[31,2048]{1,0:T(8,128)}) async-done(((f32[1024,2048]{1,0:T(8,128)}, f32[31,2048]{1,0:T(8,128)}), (f32[1024,2048]{1,0:T(8,128)}, f32[31,2048]{1,0:T(8,128)})) %all-reduce.4.cloned.1.call-update) | async-done | bytes 8642576
  (153 shorter events, 73.1 us)
Async XLA Ops:
  7.2 64.0 %all-gather.12.cloned.1.call-start = ((), (), s32[]{:S(2)}) async-start(), calls=%async_computation.1 | async-start | bytes 2359296 | tf_op jit(solution)/shard_map/all_gather | solution.py:95
  7.9 132.4 %all-gather.14.cloned.1.call-start = ((), (), s32[]{:S(2)}) async-start(), calls=%async_computation.2 | async-start | bytes 2359296 | tf_op jit(solution)/shard_map/all_gather | solution.py:96
  8.6 186.2 %all-gather.16.cloned.1.call-start = ((), (), s32[]{:S(2)}) async-start(), calls=%async_computation.3 | async-start | bytes 2359296 | tf_op jit(solution)/shard_map/all_gather | solution.py:160
  9.4 304.2 %all-gather.18.cloned.1.call-start = ((), (), s32[]{:S(2)}) async-start(), calls=%async_computation.4 | async-start | bytes 4210688 | tf_op jit(solution)/shard_map/all_gather | solution.py:92
  10.0 421.7 %all-gather.10.cloned.1.call-start = ((), (), s32[]{:S(2)}) async-start(), calls=%async_computation | async-start | bytes 2359296 | tf_op jit(solution)/shard_map/all_gather | solution.py:161
  74.8 4.8 copy-start.2
  140.3 2.9 copy-start.24
  323.4 9.3 %copy-start.22 = (bf16[31,2048]{1,0:T(8,128)(2,1)S(1)}, bf16[31,2048]{1,0:T(8,128)(2,1)}, u32[]{:S(2)}) copy-start(bf16[31,2048]{1,0:T(8,128)(2,1)} %param.10) | copy-start | bytes 380932
  323.4 9.3 %copy-start.26 = (bf16[1,128,2048]{2,1,0:T(8,128)(2,1)S(1)}, bf16[1,128,2048]{2,1,0:T(8,128)(2,1)}, u32[]{:S(2)}) copy-start(bf16[1,128,2048]{2,1,0:T(8,128)(2,1)} %param.11) | copy-start | bytes 1572868
  323.4 9.1 %collective-permute-start.1 = (bf16[1,15,2048]{2,1,0:T(8,128)(2,1)S(1)}, bf16[1,15,2048]{2,1,0:T(8,128)(2,1)S(1)}, u32[]{:S(2)}, u32[]{:S(2)}) collective-permute-start(bf16[1,15,2048]{2,1,0:T(8,128)(2,1)S(1)} %get-tuple-element.23), channel_id=1, source_target_pairs={{32,0},{64,32},{96,64},{128,96},{160,128},{192,160},{224,192},{33,... | collective-permute-start | bytes 184328 | tf_op jit(solution)/shard_map/ppermute | solution.py:22
  324.9 7.6 %collective-permute-start = (bf16[1,15,2048]{2,1,0:T(8,128)(2,1)S(1)}, bf16[1,15,2048]{2,1,0:T(8,128)(2,1)S(1)}, u32[]{:S(2)}, u32[]{:S(2)}) collective-permute-start(bf16[1,15,2048]{2,1,0:T(8,128)(2,1)S(1)} %get-tuple-element.22), channel_id=1, source_target_pairs={{0,32},{32,64},{64,96},{96,128},{128,160},{160,192},{192,224},{1,3... | collective-permute-start | bytes 184328 | tf_op jit(solution)/shard_map/ppermute | solution.py:20
  341.1 17.2 %collective-permute-start.3 = (bf16[1,15,2048]{2,0,1:T(2,128)(2,1)S(1)}, bf16[1,15,2048]{2,0,1:T(2,128)(2,1)S(1)}, u32[]{:S(2)}, u32[]{:S(2)}) collective-permute-start(bf16[1,15,2048]{2,0,1:T(2,128)(2,1)S(1)} %get-tuple-element.21), channel_id=1, source_target_pairs={{32,0},{64,32},{96,64},{128,96},{160,128},{192,160},{224,192},{33,... | collective-permute-start | bytes 184328 | tf_op jit(solution)/shard_map/ppermute | solution.py:22
  342.4 15.9 %collective-permute-start.2 = (bf16[1,15,2048]{2,0,1:T(2,128)(2,1)S(1)}, bf16[1,15,2048]{2,0,1:T(2,128)(2,1)S(1)}, u32[]{:S(2)}, u32[]{:S(2)}) collective-permute-start(bf16[1,15,2048]{2,0,1:T(2,128)(2,1)S(1)} %get-tuple-element.20), channel_id=1, source_target_pairs={{0,32},{32,64},{64,96},{96,128},{128,160},{160,192},{192,224},{1,3... | collective-permute-start | bytes 184328 | tf_op jit(solution)/shard_map/ppermute | solution.py:20
  358.3 5.9 copy-start
  370.8 347.0 %all-reduce.4.cloned.1.call-start = ((), (), s32[]{:S(2)}) async-start(), calls=%async_computation.5 | async-start | bytes 17301504
  374.0 2.7 copy-start.5
  374.0 2.7 copy-start.28
  387.2 44.4 %copy-start.12 = (f32[1024,128]{1,0:T(8,128)S(1)}, f32[1024,128]{1,0:T(8,128)}, u32[]{:S(2)}) copy-start(f32[1024,128]{1,0:T(8,128)} %fusion.8) | copy-start | bytes 1572868
  387.2 44.4 %copy-start.21 = (bf16[1,128,1024]{2,1,0:T(8,128)(2,1)S(1)}, bf16[1,128,1024]{2,1,0:T(8,128)(2,1)}, u32[]{:S(2)}) copy-start(bf16[1,128,1024]{2,1,0:T(8,128)(2,1)} %param.8) | copy-start | bytes 786436
  388.2 45.7 %copy-start.13 = (f32[1024,128]{1,0:T(8,128)S(1)}, f32[1024,128]{1,0:T(8,128)}, u32[]{:S(2)}) copy-start(f32[1024,128]{1,0:T(8,128)} %fusion.12) | copy-start | bytes 1572868
  431.6 4.4 copy-start.1
  450.9 2.7 copy-start.16
  451.2 2.7 copy-start.17
  451.5 2.7 copy-start.18
  (16 other events, 28.6 us)
Sparse Core Ops, SparseCore 0:
  10.6 60.5 all-gather.11
  73.8 59.5 all-gather.13
  136.0 58.8 all-gather.15
  198.5 115.0 all-gather.17
  370.9 60.7 all-gather.9
  437.2 280.5 all-reduce.3
where the time goes:
time: 729 us; the launch traced here: 728 us
  waiting for transfers between devices  486 us (67%)
  matrix products  95.1 us (13%)
  blocking collectives  86.5 us (12%)
  local copies, waits for them, and re-layouts  24.2 us (3%)
  starting transfers between devices  14.8 us (2%)
  between operations  14.6 us (2%)
    unnamed x7, waiting for transfers between devices  265 us
    all_gather x1, waiting for transfers between devices, shards(): lax.all_gather(out_weight, ('fsdp', 'frame'), axis=0, tiled=True)  109 us
    all_gather x1, waiting for transfers between devices, shards(): lax.all_gather(own_keys, 'fsdp', axis=0, tiled=True)  53.3 us
    all_gather x1, waiting for transfers between devices, shards(): lax.all_gather(own_queries, 'fsdp', axis=0, tiled=True)  49.5 us
    all_gather x1, blocking collectives, shards(): lax.all_gather(row_dot_table, 'fsdp', axis=0, tiled=True)  30.5 us
    all_gather x1, blocking collectives, shards(): lax.all_gather(row_maxes, 'fsdp', axis=0, tiled=True)  28.1 us
    all_gather x1, blocking collectives, shards(): lax.all_gather(row_totals, 'fsdp', axis=0, tiled=True)  27.9 us
    dot_general x16, matrix products, head_scores(): jnp.einsum('qd,kd->qk', queries, key_rows, preferred_element_type=jnp.flo...  21.8 us
  transfers between devices with their start and end apart: 10, of which 5 were waited for; matrix products, arithmetic and copies ran while one was open for 12% of the time, Pallas kernels for 0%

commit v1 on v0

--- a/solution.py
+++ b/solution.py
@@ -7,6 +7,11 @@
 HEADS = 8
 HDIM = 128
 KERNEL = 31
+
+
+def swapped_in(x, axis, dim):
+    sent = jnp.stack([x] * lax.axis_size(axis))
+    return jnp.concatenate(lax.all_to_all(sent, axis, 0, 0), axis=dim)
 
 
 def with_halo(cells, sides, width):
@@ -92,7 +97,7 @@
     full_weight = lax.all_gather(out_weight, ("fsdp", "frame"), axis=0, tiled=True)
     groups = lax.axis_size("fsdp")
     all_keys, all_values = (
-        lax.all_gather(own_keys, "fsdp", axis=0, tiled=True),
+        swapped_in(own_keys, "fsdp", 0),
         lax.all_gather(own_values, "fsdp", axis=0, tiled=True),
     )
     pieces = []

time: 729 us -> 680 us (0.933)
  waiting for transfers between devices: 486 us -> 428 us
    all_gather x1 -> x0, waiting for transfers between devices: 53.3 us -> none  [shards(): lax.all_gather(own_keys, 'fsdp', axis=0, tiled=True)]
    all_gather x1, waiting for transfers between devices: 49.5 us -> 18.9 us  [shards(): lax.all_gather(own_queries, 'fsdp', axis=0, tiled=True)]
    all_to_all x0 -> x1, waiting for transfers between devices: none -> 26.6 us  [swapped_in(): return jnp.concatenate(lax.all_to_all(sent, axis, 0, 0), axis=dim)]
    unnamed x65 -> x179, local copies, waits for them, and re-layouts: 15.9 us -> 17.2 us
    unnamed x7 -> x6, waiting for transfers between devices: 265 us -> 264 us
  transfers between devices with their start and end apart: 10 -> 10, of which waited for: 5 -> 5; matrix products, arithmetic and copies ran while one was open for 12% -> 13% of each run, Pallas kernels for 0% -> 0%
where the time goes in v1:
time: 680 us; the launch traced here: 679 us
  waiting for transfers between devices  428 us (63%)
  matrix products  95 us (14%)
  blocking collectives  86.3 us (13%)
  local copies, waits for them, and re-layouts  26.4 us (4%)
  starting transfers between devices  21.5 us (3%)
  between operations  14.8 us (2%)
    unnamed x6, waiting for transfers between devices  264 us
    all_gather x1, waiting for transfers between devices, shards(): lax.all_gather(out_weight, ('fsdp', 'frame'), axis=0, tiled=True)  109 us
    all_gather x1, blocking collectives, shards(): lax.all_gather(row_dot_table, 'fsdp', axis=0, tiled=True)  30.4 us
    all_gather x1, blocking collectives, shards(): lax.all_gather(row_totals, 'fsdp', axis=0, tiled=True)  27.9 us
    all_gather x1, blocking collectives, shards(): lax.all_gather(row_maxes, 'fsdp', axis=0, tiled=True)  27.9 us
    all_to_all x1, waiting for transfers between devices, swapped_in(): return jnp.concatenate(lax.all_to_all(sent, axis, 0, 0), axis=dim)  26.6 us
    dot_general x16, matrix products, head_scores(): jnp.einsum('qd,kd->qk', queries, key_rows, preferred_element_type=jnp.flo...  22.6 us
    conv_general_dilated x3, matrix products, depthwise(): lax.conv_general_dilated(signal[None], taps[:, None, :], (1,), 'VALID', d...  20.4 us
  transfers between devices with their start and end apart: 10, of which 5 were waited for; matrix products, arithmetic and copies ran while one was open for 13% of the time, Pallas kernels for 0%

profile of v1, /device:TPU:97, one launch (start us, length us, event | category | flops | bytes accessed | tf_op | source)
XLA Modules:
  0.0 678.9 jit_solution(17640064103976226637)
XLA Ops:
  8.6 2.5 stack.8
  11.2 6.8 all-to-all-start
  18.8 5.0 rev.3
  23.8 26.6 %all-to-all-done = bf16[8,128,1024]{2,1,0:T(8,128)(2,1)S(1)} async-done(((bf16[8,128,1024]{2,1,0:T(8,128)(2,1)}), bf16[8,128,1024]{2,1,0:T(8,128)(2,1)S(1)}, u32[]{:S(2)}, u32[]{:S(2)}) %all-to-all-start) | async-done | bytes 2097184 | tf_op jit(solution)/shard_map/all_to_all | solution.py:14
  64.6 27.9 %all_gather.25 = f32[1024,8]{0,1:T(8,128)S(1)} all-gather(f32[128,8]{0,1:T(8,128)S(1)} %stack.10), channel_id=1, replica_groups=mesh['fsdp'=8,'frame'=32] {'fsdp'}, dimensions={0}, use_global_device_ids=true | all-gather | bytes 36864 | tf_op jit(solution)/shard_map/all_gather | solution.py:170
  92.5 27.9 %all_gather.24 = f32[1024,8]{0,1:T(8,128)S(1)} all-gather(f32[128,8]{0,1:T(8,128)S(1)} %stack.9), channel_id=1, replica_groups=mesh['fsdp'=8,'frame'=32] {'fsdp'}, dimensions={0}, use_global_device_ids=true | all-gather | bytes 36864 | tf_op jit(solution)/shard_map/all_gather | solution.py:169
  127.0 18.9 %all-gather.12.cloned.1.call-done = bf16[1,1024,1024]{2,1,0:T(8,128)(2,1)} async-done(((bf16[1,128,1024]{2,1,0:T(8,128)(2,1)}), bf16[1,1024,1024]{2,1,0:T(8,128)(2,1)}) %all-gather.12.cloned.1.call-update) | async-done | bytes 2097168 | tf_op jit(solution)/shard_map/all_gather | solution.py:165
  146.0 2.3 fusion.8
  156.2 108.7 %all-gather.14.cloned.1.call-done = bf16[256,4,2048]{2,1,0:T(4,128)(2,1)} async-done(((bf16[1,4,2048]{2,1,0:T(4,128)(2,1)}), bf16[256,4,2048]{2,1,0:T(4,128)(2,1)}) %all-gather.14.cloned.1.call-update) | async-done | bytes 4194320 | tf_op jit(solution)/shard_map/all_gather | solution.py:97
  264.9 6.9 %reshape.109 = bf16[1024,2048]{1,0:T(8,128)(2,1)} reshape(bf16[256,4,2048]{2,1,0:T(4,128)(2,1)} %all-gather.14.cloned.1.call-done) | data formatting | bytes 8388608
  271.8 2.9 convolution_convert_fusion
  276.2 5.5 collective-permute-start
  284.1 8.1 %multiply_convert_fusion = (bf16[1,128,2048]{2,0,1:T(2,128)(2,1)S(1)}, f32[1,128,2048]{2,0,1:T(1,128)S(1)}) fusion(bf16[1,128,2048]{2,1,0:T(8,128)(2,1)S(1)} %copy-done.83, bf16[31,1,2048]{2,0,1:T(8,128)(2,1)S(1)} %bitcast.164, bf16[1,158,2048]{2,1,0:T(8,128)(2,1)S(1)} %pad_maximum_fusion), kind=kOutput, calls=%fused_computation.178 | convolution fusion | flops 18874368 | bytes 2871296 | tf_op jit(solution)/shard_map/conv_general_dilated | solution.py:77
  293.8 6.3 collective-permute-start.2
  300.2 7.4 %fusion.119 = f32[1,31,2048]{2,0,1:T(1,128)S(1)} fusion(f32[1,128,2048]{2,0,1:T(1,128)S(1)} %get-tuple-element.65, bf16[1,158,2048]{2,1,0:T(8,128)(2,1)S(1)} %pad_maximum_fusion, bf16[1,128,2048]{2,1,0:T(8,128)(2,1)S(1)} %copy-done.83), kind=kOutput, calls=%fused_computation.176 | convolution fusion | flops 18874368 | bytes 2473984 | tf_op jit(solution)/shard_map/conv_general_dilated | solution.py:77
  309.8 4.9 fusion
  315.7 2.3 convolution_convert_fusion.1
  334.3 4.6 fusion.126
  342.8 30.4 %all_gather.27 = f32[1024,8]{0,1:T(8,128)S(1)} all-gather(f32[128,8]{0,1:T(8,128)S(1)} %stack.11), channel_id=1, replica_groups=mesh['fsdp'=8,'frame'=32] {'fsdp'}, dimensions={0}, use_global_device_ids=true | all-gather | bytes 36864 | tf_op jit(solution)/shard_map/all_gather | solution.py:171
  373.3 9.8 %all-gather.8.cloned.1.call-done = bf16[1024,1024]{1,0:T(8,128)(2,1)} async-done(((bf16[128,1024]{1,0:T(8,128)(2,1)}), bf16[1024,1024]{1,0:T(8,128)(2,1)}) %all-gather.8.cloned.1.call-update) | async-done | bytes 2097168 | tf_op jit(solution)/shard_map/all_gather | solution.py:166
  383.1 2.4 fusion.63
  385.5 2.3 fusion.65
  394.0 2.3 fusion.73
  406.9 262.3 %all-reduce.4.cloned.1.call-done = (f32[1024,2048]{1,0:T(8,128)}, f32[31,2048]{1,0:T(8,128)}) async-done(((f32[1024,2048]{1,0:T(8,128)}, f32[31,2048]{1,0:T(8,128)}), (f32[1024,2048]{1,0:T(8,128)}, f32[31,2048]{1,0:T(8,128)})) %all-reduce.4.cloned.1.call-update) | async-done | bytes 8642576
  (267 shorter events, 78.9 us)
Async XLA Ops:
  7.2 114.6 %all-gather.10.cloned.1.call-start = ((), (), s32[]{:S(2)}) async-start(), calls=%async_computation.2 | async-start | bytes 2359296 | tf_op jit(solution)/shard_map/all_gather | solution.py:101
  7.9 138.1 %all-gather.12.cloned.1.call-start = ((), (), s32[]{:S(2)}) async-start(), calls=%async_computation.3 | async-start | bytes 2359296 | tf_op jit(solution)/shard_map/all_gather | solution.py:165
  11.2 39.2 %all-to-all-start = ((bf16[8,128,1024]{2,1,0:T(8,128)(2,1)}), bf16[8,128,1024]{2,1,0:T(8,128)(2,1)S(1)}, u32[]{:S(2)}, u32[]{:S(2)}) async-start(bf16[8,128,1024]{2,1,0:T(8,128)(2,1)} %stack.8), calls=%async_computation | async-start | bytes 4194304 | tf_op jit(solution)/shard_map/all_to_all | solution.py:14
  18.0 246.9 %all-gather.14.cloned.1.call-start = ((), (), s32[]{:S(2)}) async-start(), calls=%async_computation.4 | async-start | bytes 4210688 | tf_op jit(solution)/shard_map/all_gather | solution.py:97
  18.7 364.4 %all-gather.8.cloned.1.call-start = ((), (), s32[]{:S(2)}) async-start(), calls=%async_computation.1 | async-start | bytes 2359296 | tf_op jit(solution)/shard_map/all_gather | solution.py:166
  53.0 11.6 %copy-start.43 = (f32[128]{0:T(128)}, f32[128]{0:T(128)S(1)}, u32[]{:S(2)}) copy-start(f32[128]{0:T(128)S(1)} %get-tuple-element.48) | copy-start | bytes 1540
  53.2 10.8 %copy-start.78 = (f32[128]{0:T(128)}, f32[128]{0:T(128)S(1)}, u32[]{:S(2)}) copy-start(f32[128]{0:T(128)S(1)} %fusion.132) | copy-start | bytes 1540
  54.5 10.1 %copy-start.40 = (f32[128]{0:T(128)}, f32[128]{0:T(128)S(1)}, u32[]{:S(2)}) copy-start(f32[128]{0:T(128)S(1)} %get-tuple-element.50) | copy-start | bytes 1540
  56.0 266.3 %copy-start.10 = (f32[128,1024]{1,0:T(8,128)}, f32[128,1024]{1,0:T(8,128)S(1)}, u32[]{:S(2)}) copy-start(f32[128,1024]{1,0:T(8,128)S(1)} %get-tuple-element.53) | copy-start | bytes 1572868
  57.6 266.2 %copy-start.8 = (f32[128,1024]{1,0:T(8,128)}, f32[128,1024]{1,0:T(8,128)S(1)}, u32[]{:S(2)}) copy-start(f32[128,1024]{1,0:T(8,128)S(1)} %get-tuple-element.55) | copy-start | bytes 1572868
  59.1 265.4 %copy-start.6 = (f32[128,1024]{1,0:T(8,128)}, f32[128,1024]{1,0:T(8,128)S(1)}, u32[]{:S(2)}) copy-start(f32[128,1024]{1,0:T(8,128)S(1)} %get-tuple-element.57) | copy-start | bytes 1572868
  59.4 61.7 %copy-start.66 = (f32[128]{0:T(128)}, f32[128]{0:T(128)S(1)}, u32[]{:S(2)}) copy-start(f32[128]{0:T(128)S(1)} %fusion.140) | copy-start | bytes 1540
  60.7 264.2 %copy-start.4 = (f32[128,1024]{1,0:T(8,128)}, f32[128,1024]{1,0:T(8,128)S(1)}, u32[]{:S(2)}) copy-start(f32[128,1024]{1,0:T(8,128)S(1)} %get-tuple-element.59) | copy-start | bytes 1572868
  60.9 60.8 %copy-start.63 = (f32[128]{0:T(128)}, f32[128]{0:T(128)S(1)}, u32[]{:S(2)}) copy-start(f32[128]{0:T(128)S(1)} %fusion.142) | copy-start | bytes 1540
  62.4 59.3 %copy-start.60 = (f32[128]{0:T(128)}, f32[128]{0:T(128)S(1)}, u32[]{:S(2)}) copy-start(f32[128]{0:T(128)S(1)} %fusion.144) | copy-start | bytes 1540
  271.8 9.9 %copy-start.45 = (f32[1024,1]{0,1:T(1,128)S(1)}, f32[1024,1]{0,1:T(1,128)}, u32[]{:S(2)}) copy-start(f32[1024,1]{0,1:T(1,128)} %get-tuple-element.40) | copy-start | bytes 12292
  271.8 9.9 %copy-start.46 = (f32[1024,1]{0,1:T(1,128)S(1)}, f32[1024,1]{0,1:T(1,128)}, u32[]{:S(2)}) copy-start(f32[1024,1]{0,1:T(1,128)} %get-tuple-element.32) | copy-start | bytes 12292
  274.8 9.1 %collective-permute-start.1 = (bf16[1,15,2048]{2,1,0:T(8,128)(2,1)S(1)}, bf16[1,15,2048]{2,1,0:T(8,128)(2,1)S(1)}, u32[]{:S(2)}, u32[]{:S(2)}) collective-permute-start(bf16[1,15,2048]{2,1,0:T(8,128)(2,1)S(1)} %get-tuple-element.23), channel_id=1, source_target_pairs={{32,0},{64,32},{96,64},{128,96},{160,128},{192,160},{224,192},{33,... | collective-permute-start | bytes 184328 | tf_op jit(solution)/shard_map/ppermute | solution.py:27
  276.2 7.7 %collective-permute-start = (bf16[1,15,2048]{2,1,0:T(8,128)(2,1)S(1)}, bf16[1,15,2048]{2,1,0:T(8,128)(2,1)S(1)}, u32[]{:S(2)}, u32[]{:S(2)}) collective-permute-start(bf16[1,15,2048]{2,1,0:T(8,128)(2,1)S(1)} %get-tuple-element.22), channel_id=1, source_target_pairs={{0,32},{32,64},{64,96},{96,128},{128,160},{160,192},{192,224},{1,3... | collective-permute-start | bytes 184328 | tf_op jit(solution)/shard_map/ppermute | solution.py:25
  292.5 17.2 %collective-permute-start.3 = (bf16[1,15,2048]{2,0,1:T(2,128)(2,1)S(1)}, bf16[1,15,2048]{2,0,1:T(2,128)(2,1)S(1)}, u32[]{:S(2)}, u32[]{:S(2)}) collective-permute-start(bf16[1,15,2048]{2,0,1:T(2,128)(2,1)S(1)} %get-tuple-element.21), channel_id=1, source_target_pairs={{32,0},{64,32},{96,64},{128,96},{160,128},{192,160},{224,192},{33,... | collective-permute-start | bytes 184328 | tf_op jit(solution)/shard_map/ppermute | solution.py:27
  293.8 15.9 %collective-permute-start.2 = (bf16[1,15,2048]{2,0,1:T(2,128)(2,1)S(1)}, bf16[1,15,2048]{2,0,1:T(2,128)(2,1)S(1)}, u32[]{:S(2)}, u32[]{:S(2)}) collective-permute-start(bf16[1,15,2048]{2,0,1:T(2,128)(2,1)S(1)} %get-tuple-element.20), channel_id=1, source_target_pairs={{0,32},{32,64},{64,96},{96,128},{128,160},{160,192},{192,224},{1,3... | collective-permute-start | bytes 184328 | tf_op jit(solution)/shard_map/ppermute | solution.py:25
  322.3 346.9 %all-reduce.4.cloned.1.call-start = ((), (), s32[]{:S(2)}) async-start(), calls=%async_computation.5 | async-start | bytes 17301504
  338.9 44.2 %copy-start.32 = (bf16[1,128,1024]{2,1,0:T(8,128)(2,1)S(1)}, bf16[1,128,1024]{2,1,0:T(8,128)(2,1)}, u32[]{:S(2)}) copy-start(bf16[1,128,1024]{2,1,0:T(8,128)(2,1)} %param.8) | copy-start | bytes 786436
  340.9 46.9 %copy-start.23 = (f32[1024,128]{1,0:T(8,128)S(1)}, f32[1024,128]{1,0:T(8,128)}, u32[]{:S(2)}) copy-start(f32[1024,128]{1,0:T(8,128)} %fusion.16) | copy-start | bytes 1572868
  (73 other events, 230.1 us)
Sparse Core Ops, SparseCore 0:
  10.6 73.7 all-gather.9
  87.1 58.8 all-gather.11
  149.7 115.1 all-gather.13
  322.4 60.6 all-gather.7
  388.6 280.5 all-reduce.3
